TPU v7x, 256 devices: a whole 4x4x8 slice. The times are simulated.
256 devices in a mesh: prompt: 8 (over x_lo, y), resp: 32 (over x_hi, z, core).
Axes of the slice: x: 4 (x_hi: 2, x_lo: 2; x = x_hi * 2 + x_lo), y: 4, z: 8, core: 2. Of those that a mesh axis runs over, the one named last changes fastest.
Arguments:
- question_key_matrix: bfloat16 [32, 2048, 256], P('resp', 'prompt'), may hold values from -0.31835938 to 0.31835938
- prompt_values: bfloat16 [32, 2048, 256], P('resp', 'prompt'), may hold values from -6 to 6
- prompt_gates: float32 [32, 2, 2048], P('resp', None, 'prompt'), may hold values from -2.3 to 0, as said below
- resp_queries: bfloat16 [1024, 512, 256], P(('prompt', 'resp')), may hold values from -0.31835938 to 0.31835938
- resp_keys: bfloat16 [1024, 512, 256], P(('prompt', 'resp')), may hold values from -0.31835938 to 0.31835938
- response_value_rows: bfloat16 [1024, 512, 256], P(('prompt', 'resp')), may hold values from -6 to 6
- resp_gates: float32 [1024, 2, 512], P(('prompt', 'resp')), may hold values from -2.3 to 0, as said below
- resp_cotangent: bfloat16 [1024, 512, 256], P(('prompt', 'resp')), may hold values from -0.59765625 to 0.59765625
- group_ids: int32 [1024], P(('prompt', 'resp')), may hold values from 0 to 31, as said below
- resp_lengths: int32 [256, 4], P(('prompt', 'resp')), may hold values from 1 to 512, 1536 in all within a row
- loss_mask: int32 [1024, 512], P(('prompt', 'resp')), may hold values 0 or 1
- advantages: int32 [1024], P(('prompt', 'resp')), may hold values from -2048 to 2048
Outputs:
- resp_out: bfloat16 [1024, 512, 256], P(('prompt', 'resp'))
- resp_dq: bfloat16 [1024, 512, 256], P(('prompt', 'resp'))
- answer_key_derivative: bfloat16 [1024, 512, 256], P(('prompt', 'resp'))
- resp_dv: bfloat16 [1024, 512, 256], P(('prompt', 'resp'))
- prompt_dk: bfloat16 [32, 2048, 256], P('resp', 'prompt')
- prompt_dv: bfloat16 [32, 2048, 256], P('resp', 'prompt')
Inputs may be any that keep to these rules, and one draw needn't show every extreme that they name: `group_ids`: never falling along the responses; every prompt has at least one response. `resp_lengths`: the lengths of one device's 4 responses sum to 1536. `prompt_gates`: negative log decays. `resp_gates`: negative log decays.
All inputs are finite; a program needn't handle non-finite values. No bound on the sum of `loss_mask` on one device may be relied on, other than what follows from the above.
Results may differ from a plain program's by a relative error of at most 0.012.
Values may be sent and summed in bfloat16 or wider, within the bound.
A program may use at most 64 MiB of HBM per device.

v0:
```python
import jax
import jax.numpy as jnp
from jax import lax
from jax.sharding import PartitionSpec as P

H = 2
DH = 128
RMAX = 512


def carried_in(x, axis, combine, identity):
    count, place = (lax.axis_size(axis), lax.axis_index(axis))
    everything = jax.tree.map(lambda part: lax.all_gather(part, axis), x)
    start = jax.tree.map(
        lambda part, zero: jnp.broadcast_to(jnp.asarray(zero, part.dtype), part.shape), x, identity
    )

    def hop(k, before):
        reached = k < place
        new = combine(before, jax.tree.map(lambda part: part[k], everything))
        return jax.tree.map(lambda a, b: jnp.where(reached, a, b), new, before)

    return lax.fori_loop(0, count, hop, start)


def from_root(x, axis, root):
    mine = lax.axis_index(axis) == root
    return lax.psum(jnp.where(mine, x, jnp.zeros_like(x)), axis)


def head_pass(query_h, key_h, value_h, gate_h, start_h, cot_h, weight, live_rows, open_rows):
    cum_gate = jnp.cumsum(gate_h)
    places = jnp.arange(gate_h.shape[0])
    causal = places[:, None] >= places[None, :]
    decay = jnp.where(
        causal, jnp.exp(jnp.where(causal, cum_gate[:, None] - cum_gate[None, :], 0.0)), 0.0
    )
    carried = jnp.exp(cum_gate)[:, None]
    scores = jnp.dot(query_h, key_h.T, preferred_element_type=jnp.float32)
    mixing = (scores * decay).astype(jnp.bfloat16)
    output = carried * jnp.dot(query_h, start_h, preferred_element_type=jnp.float32)
    output = (output + jnp.dot(mixing, value_h, preferred_element_type=jnp.float32)) * open_rows[
        :, None
    ]
    grad_out = (cot_h.astype(jnp.float32) * (live_rows * weight)[:, None]).astype(jnp.bfloat16)
    grad_mix = jnp.dot(grad_out, value_h.T, preferred_element_type=jnp.float32)
    grad_scores = (grad_mix * decay).astype(jnp.bfloat16)
    grad_query = jnp.dot(grad_scores, key_h, preferred_element_type=jnp.float32)
    grad_query = grad_query + carried * jnp.dot(
        grad_out, start_h.T, preferred_element_type=jnp.float32
    )
    grad_key = jnp.dot(grad_scores.T, query_h, preferred_element_type=jnp.float32)
    grad_value = jnp.dot(mixing.T, grad_out, preferred_element_type=jnp.float32)
    scaled_out = (carried * grad_out.astype(jnp.float32)).astype(jnp.bfloat16)
    opening_memory_derivative = jnp.dot(query_h.T, scaled_out, preferred_element_type=jnp.float32)
    return (output, grad_query, grad_key, grad_value, opening_memory_derivative)


def response_sweep(queries, keys_in, values, gates, start, cotangent, weight, live_rows, open_rows):
    width = start.shape[1]
    pieces = []
    for head_index in range(start.shape[0]):
        lower = head_index * width
        upper = lower + width
        pieces.append(
            head_pass(
                queries[:, lower:upper],
                keys_in[:, lower:upper],
                values[:, lower:upper],
                gates[head_index],
                start[head_index],
                cotangent[:, lower:upper],
                weight,
                live_rows,
                open_rows,
            )
        )
    joined = [
        jnp.concatenate([entry[slot] for entry in pieces], axis=1).astype(jnp.bfloat16)
        for slot in range(4)
    ]
    opening_memory_derivative = jnp.stack([entry[4] for entry in pieces])
    return (joined[0], joined[1], joined[2], joined[3], opening_memory_derivative)


def chain_join(earlier, later):
    return (earlier[0] + later[0], jnp.exp(later[0])[:, None, None] * earlier[1] + later[1])


def shards(
    question_key_matrix,
    prompt_values,
    prompt_gates,
    resp_queries,
    resp_keys,
    response_value_rows,
    resp_gates,
    resp_cotangent,
    group_ids,
    resp_lengths,
    loss_mask,
    advantages,
):
    gates = prompt_gates[0]
    piece_log = jnp.sum(gates, axis=1)
    suffix = jnp.cumsum(gates[:, ::-1], axis=1)[:, ::-1] - gates
    key_f = question_key_matrix[0].astype(jnp.float32)
    value_f = prompt_values[0].astype(jnp.float32)
    local_list = []
    for head_index in range(H):
        lower = head_index * DH
        local_list.append(
            jnp.dot(
                key_f[:, lower : lower + DH].T,
                jnp.exp(suffix[head_index])[:, None] * value_f[:, lower : lower + DH],
                precision=lax.Precision.HIGHEST,
            )
        )
    local_state = jnp.stack(local_list)
    blank = (jnp.zeros_like(piece_log), jnp.zeros_like(local_state))
    before_log, start_state = carried_in((piece_log, local_state), "prompt", chain_join, blank)
    final_state = (jnp.exp(piece_log)[:, None, None] * start_state + local_state).astype(
        jnp.bfloat16
    )
    last_row = lax.axis_size("prompt") - 1
    gathered = lax.all_gather(final_state[None], "resp", axis=0, tiled=True)
    gathered = from_root(gathered, "prompt", last_row)
    lengths = resp_lengths[0]
    places = jnp.arange(RMAX)
    open_rows = (places[None, :] < lengths[:, None]).astype(jnp.float32)
    live_rows = loss_mask.astype(jnp.float32) * open_rows
    weights = advantages.astype(jnp.float32) / 1024.0
    starts = jnp.take(gathered, group_ids, axis=0)

    def resp_item(item):
        return response_sweep(
            item[0], item[1], item[2], item[3], item[4], item[5], item[6], item[7], item[8]
        )

    outs = lax.map(
        resp_item,
        (
            resp_queries,
            resp_keys,
            response_value_rows,
            resp_gates,
            starts,
            resp_cotangent,
            weights,
            live_rows,
            open_rows,
        ),
    )
    prompts = gathered.shape[0]
    one_hot = (group_ids[:, None] == jnp.arange(prompts)[None, :]).astype(jnp.float32)
    grad_flat = outs[4].reshape(outs[4].shape[0], -1)
    contrib = jnp.dot(one_hot.T, grad_flat, precision=lax.Precision.HIGHEST).reshape(gathered.shape)
    summed, total_log = lax.psum((contrib, piece_log), "prompt")
    owned = lax.psum_scatter(summed, "resp", scatter_dimension=0, tiled=True)
    grad_final = owned[0]
    later_log = total_log - before_log - piece_log
    factor = jnp.exp(suffix + later_log[:, None])
    grad_keys = []
    grad_values = []
    for head_index in range(H):
        lower = head_index * DH
        scale_rows = factor[head_index][:, None]
        grad_keys.append(
            scale_rows
            * jnp.dot(
                value_f[:, lower : lower + DH],
                grad_final[head_index].T,
                precision=lax.Precision.HIGHEST,
            )
        )
        grad_values.append(
            scale_rows
            * jnp.dot(
                key_f[:, lower : lower + DH],
                grad_final[head_index],
                precision=lax.Precision.HIGHEST,
            )
        )
    prompt_dk = jnp.concatenate(grad_keys, axis=1).astype(jnp.bfloat16)
    prompt_dv = jnp.concatenate(grad_values, axis=1).astype(jnp.bfloat16)
    return (outs[0], outs[1], outs[2], outs[3], prompt_dk[None], prompt_dv[None])


def solution(mesh):
    placed = (
        P("resp", "prompt", None),
        P("resp", "prompt", None),
        P("resp", None, "prompt"),
        P(("prompt", "resp"), None, None),
        P(("prompt", "resp"), None, None),
        P(("prompt", "resp"), None, None),
        P(("prompt", "resp"), None, None),
        P(("prompt", "resp"), None, None),
        P(("prompt", "resp")),
        P(("prompt", "resp"), None),
        P(("prompt", "resp"), None),
        P(("prompt", "resp")),
    )
    return jax.shard_map(
        shards,
        mesh=mesh,
        in_specs=placed,
        out_specs=(
            P(("prompt", "resp"), None, None),
            P(("prompt", "resp"), None, None),
            P(("prompt", "resp"), None, None),
            P(("prompt", "resp"), None, None),
            P("resp", "prompt", None),
            P("resp", "prompt", None),
        ),
        check_vma=False,
    )
```

profile of v0, /device:TPU:1, one launch (start us, length us, event | category | flops | bytes accessed | tf_op | source)
XLA Modules:
  0.0 519.6 jit_solution(12558712208117287017)
XLA Ops:
  10.9 1.2 convolution_bitcast_fusion.2
  12.1 1.2 convolution_bitcast_fusion.3
  15.0 1.3 dynamic-slice
  17.2 17.3 %all-reduce.1 = (f32[16]{0:T(128)S(1)}, f32[2]{0:T(128)S(1)}) all-reduce(f32[16]{0:T(128)S(1)} %dynamic-update-slice, f32[2]{0:T(128)S(1)} %reduce_sum.9), channel_id=2, replica_groups=mesh['prompt'=8,'resp'=32] {'prompt'}, use_global_device_ids=true, to_apply=%add | all-reduce | flops 18 | bytes 144
  34.6 19.7 %all-gather.6.cloned.1.call-done = f32[16,128,128]{2,1,0:T(8,128)} async-done(((f32[2,128,128]{2,1,0:T(8,128)}), f32[16,128,128]{2,1,0:T(8,128)}) %all-gather.6.cloned.1.call-update) | async-done | bytes 1048592 | tf_op jit(solution)/shard_map/all_gather | solution.py:13
  54.3 8.3 %while.35 = (s32[]{:T(128)}, f32[2]{0:T(128)S(1)}, f32[2,128,128]{2,1,0:T(8,128)S(1)}, s32[]{:T(128)}, f32[8,2]{1,0:T(8,128)S(1)}, /*index=5*/f32[8,2,128,128]{3,2,1,0:T(8,128)}, s32[]{:T(128)}, s32[]{:T(128)}) while((s32[]{:T(128)}, f32[2]{0:T(128)S(1)}, f32[2,128,128]{2,1,0:T(8,128)S(1)}, s32[]{:T(128)}, f32[8,2]{1,0:T(8,128)S(1)}, ...), condition=%wide.region_4.5_spmd.clone, body=%wide.region_3.4_spmd.clone.sunk | while | flops 131082 | bytes 393379 | solution.py:23
  56.4 1.0 fusion.163
  63.6 84.7 %all-gather.8.cloned.1.call-done = bf16[64,128,128]{2,1,0:T(8,128)(2,1)} async-done(((bf16[2,128,128]{2,1,0:T(8,128)(2,1)}), bf16[64,128,128]{2,1,0:T(8,128)(2,1)}) %all-gather.8.cloned.1.call-update) | async-done | bytes 2097168 | tf_op jit(solution)/shard_map/all_gather | solution.py:126
  148.3 1.5 broadcast_select_fusion.2
  150.7 80.2 %all-reduce.5.cloned.1.call-done = bf16[32,2,128,128]{3,2,1,0:T(8,128)(2,1)} async-done(((bf16[32,2,128,128]{3,2,1,0:T(8,128)(2,1)}), bf16[32,2,128,128]{3,2,1,0:T(8,128)(2,1)}) %all-reduce.5.cloned.1.call-update) | async-done | bytes 2097168 | tf_op jit(solution)/shard_map/psum | solution.py:28
  230.9 2.2 gather_fusion
  233.2 59.8 %while.34 = (s32[]{:T(128)}, bf16[4,512,256]{2,1,0:T(8,128)(2,1)}, bf16[4,512,256]{2,1,0:T(8,128)(2,1)}, bf16[4,512,256]{2,1,0:T(8,128)(2,1)}, bf16[4,512,256]{2...) while((s32[]{:T(128)}, bf16[4,512,256]{2,1,0:T(8,128)(2,1)}, ...), condition=%wide.region_11.12_spmd, body=%wide.region_6.11_spmd.sunk | while | flops 917668352 | bytes 22106636 | solution.py:140
  239.5 1.1 dynamic-slice_bitcast_fusion.20
  254.5 1.1 dynamic-slice_bitcast_fusion.20
  269.4 1.1 dynamic-slice_bitcast_fusion.20
  284.4 1.1 dynamic-slice_bitcast_fusion.20
  293.4 2.0 fusion.65
  295.4 4.4 copy.41
  299.9 127.3 %reduce-scatter.2.cloned.1.call-done = f32[1,2,128,128]{3,2,1,0:T(8,128)} async-done(((f32[32,2,128,128]{3,2,1,0:T(8,128)}), f32[1,2,128,128]{3,2,1,0:T(8,128)}) %reduce-scatter.2.cloned.1.call-update) | async-done | bytes 131088 | tf_op jit(solution)/shard_map/reduce_scatter | solution.py:159
  427.3 79.8 %all-reduce.7.cloned.1.call-done = f32[1,2,128,128]{3,2,1,0:T(8,128)} async-done(((f32[1,2,128,128]{3,2,1,0:T(8,128)}), f32[1,2,128,128]{3,2,1,0:T(8,128)}) %all-reduce.7.cloned.1.call-update) | async-done | bytes 131088 | tf_op jit(solution)/shard_map/psum | solution.py:158
  507.1 1.1 fusion.53
  508.2 1.1 fusion.54
  510.0 1.1 fusion.51
  511.1 1.1 fusion.52
  (267 shorter events, 71.3 us)
Async XLA Ops:
  7.2 47.1 %all-gather.6.cloned.1.call-start = ((), (), s32[]{:S(2)}) async-start(), calls=%async_computation.2 | async-start | bytes 1179648 | tf_op jit(solution)/shard_map/all_gather | solution.py:13
  14.1 134.2 %all-gather.8.cloned.1.call-start = ((), (), s32[]{:S(2)}) async-start(), calls=%async_computation.3 | async-start | bytes 2162688 | tf_op jit(solution)/shard_map/all_gather | solution.py:126
  63.6 167.3 %all-reduce.5.cloned.1.call-start = ((), (), s32[]{:S(2)}) async-start(), calls=%async_computation.1 | async-start | bytes 4194304 | tf_op jit(solution)/shard_map/psum | solution.py:28
  149.8 0.7 copy-start.4
  149.8 0.7 copy-start.5
  149.8 0.7 copy-start.3
  149.8 0.8 copy-start.2
  149.9 277.4 %reduce-scatter.2.cloned.1.call-start = ((), (), s32[]{:S(2)}) async-start(), calls=%async_computation.4 | async-start | bytes 4325376 | tf_op jit(solution)/shard_map/reduce_scatter | solution.py:159
  299.7 207.4 %copy-start = (bf16[1,256,256]{2,1,0:T(8,128)(2,1)S(1)}, bf16[1,256,256]{2,1,0:T(8,128)(2,1)}, u32[]{:S(2)}) copy-start(bf16[1,256,256]{2,1,0:T(8,128)(2,1)} %param.17) | copy-start | bytes 393220
  299.7 210.3 %copy-start.1 = (bf16[1,256,256]{2,1,0:T(8,128)(2,1)S(1)}, bf16[1,256,256]{2,1,0:T(8,128)(2,1)}, u32[]{:S(2)}) copy-start(bf16[1,256,256]{2,1,0:T(8,128)(2,1)} %param.16) | copy-start | bytes 393220
  299.8 207.3 %all-reduce.7.cloned.1.call-start = ((), (), s32[]{:S(2)}) async-start(), calls=%async_computation.5 | async-start | bytes 262144 | tf_op jit(solution)/shard_map/psum | solution.py:158
Sparse Core Ops, SparseCore 0:
  14.2 40.0 all-gather.5
  63.7 84.5 all-gather.7
  151.0 79.8 all-reduce.4
  299.9 127.2 reduce-scatter.1
  429.7 77.3 all-reduce.6
where the time goes:
time: 525 us; the launch traced here: 520 us
  waiting for transfers between devices  392 us (75%)
  local copies, waits for them, and re-layouts  46.6 us (9%)
  matrix products  28 us (5%)
  other arithmetic  19.7 us (4%)
  blocking collectives  17.3 us (3%)
  between operations  14.7 us (3%)
    reduce_scatter x1, waiting for transfers between devices, shards(): owned = lax.psum_scatter(summed, 'resp', scatter_dimension=0, tiled=True)  127 us
    all_gather x1, waiting for transfers between devices, shards(): gathered = lax.all_gather(final_state[None], 'resp', axis=0, tiled=True)  84.7 us
    psum x1, waiting for transfers between devices, from_root(): return lax.psum(jnp.where(mine, x, jnp.zeros_like(x)), axis)  80.2 us
    psum x1, waiting for transfers between devices, shards(): summed, total_log = lax.psum((contrib, piece_log), 'prompt')  79.8 us
    all_gather x1, waiting for transfers between devices, carried_in(): everything = jax.tree.map(lambda part: lax.all_gather(part, axis), x)  19.7 us
    unnamed x1, blocking collectives  17.3 us
    dynamic_update_slice x32, local copies, waits for them, and re-layouts, shards(): lax.map(resp_item, (resp_queries, resp_keys, response_value_rows, resp_ga...  13.7 us
  transfers between devices with their start and end apart: 5, of which 5 were waited for; matrix products, arithmetic and copies ran while one was open for 1% of the time, Pallas kernels for 0%

commit v1 on v0

v1 whole, which is shorter than its diff:
```python
import functools

import jax
import jax.numpy as jnp
from jax import lax
from jax.experimental import pallas as pl
from jax.experimental.pallas import tpu as pltpu
from jax.sharding import PartitionSpec as P

H = 2
DH = 128
RMAX = 512
NR = 4
PIECE = 256
PLANE = 32
RING = 8
CH = 256
HI = lax.Precision.HIGHEST
MESH = pl.DeviceIdType.MESH
F32 = jnp.float32
BF16 = jnp.bfloat16


def mm(x, y, cx, cy, **kw):
    return lax.dot_general(x, y, (((cx,), (cy,)), ((), ())), preferred_element_type=F32, **kw)


def split(x):
    hi = x.astype(BF16)
    return hi, (x - hi.astype(F32)).astype(BF16)


def iota(shape, axis):
    return lax.broadcasted_iota(jnp.int32, shape, axis)


def exchange_kernel(
    gid, lens, adv, pk_hbm, pv_hbm, pg, q_hbm, cot_hbm, rg, mask,
    dk_out, dv_out, starts_out,
    pk, pv, q, cot, f1s, f1r, f2s, f2r, f3s, f3r, g1s, g1r, g2s, g2r, g3s, g3r, oh,
    in_sems, send_sems, recv_sems,
):
    a = lax.axis_index("prompt")
    b = lax.axis_index("resp")
    quad = lax.div(b, 16) * 2 + lax.rem(b, 2)
    z = lax.rem(lax.div(b, 2), RING)
    me = a * 4 + quad

    def plane_peer(k):
        j = lax.rem(me + k, PLANE)
        qj = lax.rem(j, 4)
        return j, (lax.div(j, 4), lax.div(qj, 2) * 16 + z * 2 + lax.rem(qj, 2))

    def ring_peer(k):
        zz = lax.rem(z + k, RING)
        return zz, (a, lax.div(quad, 2) * 16 + zz * 2 + lax.rem(quad, 2))

    loads = [
        pltpu.make_async_copy(s, d, in_sems.at[i])
        for i, (s, d) in enumerate(((pk_hbm, pk), (pv_hbm, pv), (q_hbm, q), (cot_hbm, cot)))
    ]
    for c in loads:
        c.start()

    barrier = pltpu.get_barrier_semaphore()

    def greet_plane(k, _):
        pl.semaphore_signal(barrier, inc=1, device_id=plane_peer(k)[1], device_id_type=MESH)
        return 0

    def greet_ring(k, _):
        pl.semaphore_signal(barrier, inc=1, device_id=ring_peer(k)[1], device_id_type=MESH)
        return 0

    lax.fori_loop(1, PLANE, greet_plane, 0)
    lax.fori_loop(1, RING, greet_ring, 0)

    def send_all(n, peer, stage, src_of, dst):
        def one(k, _):
            j, dev = peer(k)
            pltpu.make_async_remote_copy(
                src_ref=src_of(j),
                dst_ref=dst,
                send_sem=send_sems.at[stage],
                recv_sem=recv_sems.at[stage],
                device_id=dev,
                device_id_type=MESH,
            ).start()
            return 0

        lax.fori_loop(1, n, one, 0)

    def wait_all(ref, sems, stage):
        pltpu.make_async_copy(ref, ref, sems.at[stage]).wait()

    gates = jnp.concatenate([pg[0], jnp.zeros((6, PIECE), F32)], axis=0)
    later = (iota((PIECE, PIECE), 1) > iota((PIECE, PIECE), 0)).astype(F32)
    suf = mm(later, gates, 1, 1, precision=HI)
    total = jnp.sum(gates, axis=1, keepdims=True)
    loads[0].wait()
    loads[1].wait()
    for h in range(H):
        cols = slice(h * DH, (h + 1) * DH)
        hi, lo = split(jnp.exp(suf[:, h : h + 1]) * pv[0, :, cols].astype(F32))
        kh = pk[0, :, cols]
        state = mm(kh, hi, 0, 0) + mm(kh, lo, 0, 0)
        f1s[h * 16 : (h + 1) * 16, 0:8, :] = state.reshape(16, 8, DH)
    row = iota((8, DH), 0)
    meta = jnp.broadcast_to(total, (8, DH))
    for r in range(NR):
        g = gid[r]
        slot = ((g >> 1) & 7) * 4 + (g >> 4) * 2 + (g & 1)
        meta = jnp.where(row == 2 + r, (slot * 8).astype(F32), meta)
    f1s[:, 8:16, :] = jnp.broadcast_to(meta[None], (PLANE, 8, DH))
    f1r[me] = f1s[me]

    pl.semaphore_wait(barrier, PLANE - 1 + RING - 1)
    send_all(PLANE, plane_peer, 0, lambda j: f1s.at[j], f1r.at[me])

    upper = (iota((DH, DH), 0) <= iota((DH, DH), 1)).astype(F32)
    nch = RMAX // DH
    grows = jnp.concatenate(
        [rg[r, :, c * DH : (c + 1) * DH] for c in range(nch) for r in range(NR)], axis=0
    )
    grows = mm(grows, upper, 1, 0, precision=HI)
    before = jnp.zeros((8, 1), F32)
    erows = []
    for c in range(nch):
        local = grows[c * 8 : (c + 1) * 8]
        erows.append(jnp.exp(local + before))
        before = before + local[:, DH - 1 : DH]
    lane = iota((1, DH), 1)
    lrows = []
    for c in range(nch):
        for r in range(NR):
            on = mask[r : r + 1, c * DH : (c + 1) * DH].astype(F32)
            on = jnp.where(lane + c * DH < lens[0, r], on, 0.0)
            lrows.append(on * (adv[r].astype(F32) * (1.0 / 1024.0)))
    rows = jnp.concatenate(erows + lrows + [jnp.zeros((DH - 48, DH), F32)], axis=0)
    columns = rows.T
    loads[2].wait()
    loads[3].wait()
    for pair in range(NR // 2):
        for h in range(H):
            cols = slice(h * DH, (h + 1) * DH)
            found = []
            for r in (2 * pair, 2 * pair + 1):
                parts = []
                for c in range(nch):
                    live = columns[:, 32 + c * 4 + r : 33 + c * 4 + r]
                    e = columns[:, c * 8 + r * 2 + h : c * 8 + r * 2 + h + 1]
                    go = cot[r, c * DH : (c + 1) * DH, cols].astype(F32) * live
                    parts.append((go.astype(BF16).astype(F32) * e).astype(BF16))
                scaled = jnp.concatenate(parts, axis=0)
                found.append(mm(q[r, :, cols], scaled, 0, 0).reshape(16, 8, DH))
            g1s[h * 16 : (h + 1) * 16, pair * 16 : (pair + 1) * 16, :] = jnp.concatenate(
                found, axis=1
            ).astype(BF16)
    g1r[me] = g1s[me]
    send_all(PLANE, plane_peer, 3, lambda j: g1s.at[j], g1r.at[me])

    wait_all(f1r.at[pl.ds(0, PLANE - 1)], recv_sems, 0)
    data = f1r[:, 0:8, :].reshape(8, 4, 8, DH)
    logs = jnp.where(a >= 4, f1r[:, 9:10, :], f1r[:, 8:9, :]).reshape(8, 4, 1, DH)
    acc = data[7]
    run = logs[7]
    for piece in range(6, -1, -1):
        acc = acc + jnp.exp(run) * data[piece]
        run = run + logs[piece]
    f2s[...] = acc.reshape(32, DH).astype(BF16)
    f2r[z] = f2s[...]
    send_all(RING, ring_peer, 1, lambda j: f2s, f2r.at[z])

    after = jnp.zeros((8, DH), F32)
    for piece in range(8):
        after = after + jnp.where(piece > a, f1r[piece * 4 + quad, 8:16, :], 0.0)
    sub = iota((1, 8, DH), 1).astype(F32)
    wide = jnp.concatenate(
        [jnp.broadcast_to(f1r[:, 10 + r : 11 + r, :], (PLANE, 8, DH)) + sub for r in range(NR)], axis=1
    ).reshape(PLANE * 32, DH)
    lanes = iota((1, DH), 1).astype(F32)
    oh[:, 0:DH] = jnp.where(wide == lanes, 1.0, 0.0).astype(BF16)
    oh[:, DH : 2 * DH] = jnp.where(wide == lanes + float(DH), 1.0, 0.0).astype(BF16)

    wait_all(g1r.at[pl.ds(0, PLANE - 1)], recv_sems, 3)
    added = mm(oh[...], g1r[...].reshape(PLANE * 32, DH), 0, 0)
    g2s[...] = added.astype(BF16).reshape(RING, 32, DH)
    g2r[z] = g2s[z]
    send_all(RING, ring_peer, 4, lambda j: g2s.at[j], g2r.at[z])

    wait_all(f2r.at[pl.ds(0, RING - 1)], recv_sems, 1)
    picked = mm(oh[...], f2r[...].reshape(RING * 32, DH), 1, 0)
    f3s[...] = picked.astype(BF16).reshape(PLANE, 32, DH)
    f3r[me] = f3s[me]
    send_all(PLANE, plane_peer, 2, lambda j: f3s.at[j], f3r.at[me])

    wait_all(g2r.at[pl.ds(0, RING - 1)], recv_sems, 4)
    g3s[...] = jnp.sum(g2r[...].astype(F32), axis=0).reshape(4, 8, DH)
    g3r[me] = g3s[quad]
    send_all(PLANE, plane_peer, 5, lambda j: g3s.at[lax.rem(j, 4)], g3r.at[me])

    wait_all(g3r.at[pl.ds(0, PLANE - 1)], recv_sems, 5)
    for h in range(H):
        cols = slice(h * DH, (h + 1) * DH)
        factor = jnp.exp(suf[:, h : h + 1] + after[h : h + 1, 0:1])
        hi, lo = split(g3r[h * 16 : (h + 1) * 16].reshape(DH, DH))
        vh = pv[0, :, cols]
        kh = pk[0, :, cols]
        dk_out[0, :, cols] = (factor * (mm(vh, hi, 1, 1) + mm(vh, lo, 1, 1))).astype(BF16)
        dv_out[0, :, cols] = (factor * (mm(kh, hi, 1, 0) + mm(kh, lo, 1, 0))).astype(BF16)

    wait_all(f3r.at[pl.ds(0, PLANE - 1)], recv_sems, 2)
    got = f3r[...].astype(F32)
    for r in range(NR):
        starts_out[r] = got[:, r * 8 : (r + 1) * 8, :].reshape(2 * DH, DH).astype(BF16)

    wait_all(f1s.at[pl.ds(0, PLANE - 1)], send_sems, 0)
    wait_all(f2r.at[pl.ds(0, RING - 1)], send_sems, 1)
    wait_all(f3s.at[pl.ds(0, PLANE - 1)], send_sems, 2)
    wait_all(g1s.at[pl.ds(0, PLANE - 1)], send_sems, 3)
    wait_all(g2s.at[pl.ds(0, RING - 1)], send_sems, 4)
    wait_all(g3r.at[pl.ds(0, PLANE - 1)], send_sems, 5)


def exchange(gid, lens, adv, pk, pv, pg, q, cot, rg, mask):
    smem = pl.BlockSpec(memory_space=pltpu.SMEM)
    vmem = pl.BlockSpec(memory_space=pltpu.VMEM)
    anywhere = pl.BlockSpec(memory_space=pl.ANY)
    return pl.pallas_call(
        exchange_kernel,
        out_shape=(
            jax.ShapeDtypeStruct((1, PIECE, H * DH), BF16),
            jax.ShapeDtypeStruct((1, PIECE, H * DH), BF16),
            jax.ShapeDtypeStruct((NR, H * DH, DH), BF16),
        ),
        in_specs=[smem, smem, smem, anywhere, anywhere, vmem, anywhere, anywhere, vmem, vmem],
        out_specs=(vmem, vmem, vmem),
        scratch_shapes=[
            pltpu.VMEM((1, PIECE, H * DH), BF16),
            pltpu.VMEM((1, PIECE, H * DH), BF16),
            pltpu.VMEM((NR, RMAX, H * DH), BF16),
            pltpu.VMEM((NR, RMAX, H * DH), BF16),
            pltpu.VMEM((PLANE, 16, DH), F32),
            pltpu.VMEM((PLANE, 16, DH), F32),
            pltpu.VMEM((32, DH), BF16),
            pltpu.VMEM((RING, 32, DH), BF16),
            pltpu.VMEM((PLANE, 32, DH), BF16),
            pltpu.VMEM((PLANE, 32, DH), BF16),
            pltpu.VMEM((PLANE, 32, DH), BF16),
            pltpu.VMEM((PLANE, 32, DH), BF16),
            pltpu.VMEM((RING, 32, DH), BF16),
            pltpu.VMEM((RING, 32, DH), BF16),
            pltpu.VMEM((4, 8, DH), F32),
            pltpu.VMEM((PLANE, 8, DH), F32),
            pltpu.VMEM((PLANE * 32, 2 * DH), BF16),
            pltpu.SemaphoreType.DMA((4,)),
            pltpu.SemaphoreType.DMA((6,)),
            pltpu.SemaphoreType.DMA((6,)),
        ],
        compiler_params=pltpu.CompilerParams(
            collective_id=0, has_side_effects=True, vmem_limit_bytes=32 << 20
        ),
        name="exchange",
    )(gid, lens, adv, pk, pv, pg, q, cot, rg, mask)


def response_kernel(lens, adv, q_ref, k_ref, v_ref, cot_ref, rg, mask, start_ref, out_ref, dq_ref, dk_ref, dv_ref):
    r = pl.program_id(0)
    length = lens[0, r]
    weight = adv[r].astype(F32) * (1.0 / 1024.0)
    nch = RMAX // CH

    def body(chunks):
        upper = (iota((CH, CH), 0) <= iota((CH, CH), 1)).astype(F32)
        lane = iota((1, CH), 1)
        grows = jnp.concatenate(
            [rg[0, :, c * CH : (c + 1) * CH] for c in range(nch)] + [jnp.zeros((8 - 2 * nch, CH), F32)],
            axis=0,
        )
        crows = mm(grows, upper, 1, 0, precision=HI)
        lrows = []
        for c in range(nch):
            on = mask[pl.ds(r, 1), c * CH : (c + 1) * CH].astype(F32)
            lrows.append(jnp.where(lane + c * CH < length, on, 0.0) * weight)
        rows = jnp.concatenate([crows] + lrows + [jnp.zeros((DH - 8 - nch, CH), F32)], axis=0)
        columns = rows.T
        causal = iota((CH, CH), 0) >= iota((CH, CH), 1)
        place = iota((CH, 1), 0)
        for h in range(H):
            cols = slice(h * DH, (h + 1) * DH)
            state = start_ref[0, cols, :]
            q, k, v, go, col, tot = [], [], [], [], [], []
            for c in range(chunks):
                tok = slice(c * CH, (c + 1) * CH)
                q.append(q_ref[0, tok, cols])
                k.append(k_ref[0, tok, cols])
                v.append(v_ref[0, tok, cols])
                live = columns[:, 8 + c : 9 + c]
                go.append((cot_ref[0, tok, cols].astype(F32) * live).astype(BF16))
                col.append(columns[:, 2 * c + h : 2 * c + h + 1])
                tot.append(crows[2 * c + h : 2 * c + h + 1, CH - 1 : CH])
            back = [None] * chunks
            for c in range(chunks - 1, 0, -1):
                scaled = (jnp.exp(col[c]) * go[c].astype(F32)).astype(BF16)
                grad = mm(q[c], scaled, 0, 0)
                if back[c] is not None:
                    grad = grad + jnp.exp(tot[c]) * back[c]
                back[c - 1] = grad
            for c in range(chunks):
                tok = slice(c * CH, (c + 1) * CH)
                e = jnp.exp(col[c])
                f = jnp.exp(tot[c] - col[c])
                decay = jnp.exp(
                    jnp.where(causal, col[c] - crows[2 * c + h : 2 * c + h + 1, :], -1e30)
                )
                mix = (mm(q[c], k[c], 1, 1) * decay).astype(BF16)
                gs = (mm(go[c], v[c], 1, 1) * decay).astype(BF16)
                sb = state.astype(BF16)
                out = e * mm(q[c], sb, 1, 0) + mm(mix, v[c], 1, 0)
                out_ref[0, tok, cols] = jnp.where(place + c * CH < length, out, 0.0).astype(BF16)
                dq_ref[0, tok, cols] = (e * mm(go[c], sb, 1, 1) + mm(gs, k[c], 1, 0)).astype(BF16)
                dk = mm(gs, q[c], 0, 0)
                dv = mm(mix, go[c], 0, 0)
                if back[c] is not None:
                    bb = back[c].astype(BF16)
                    dk = dk + f * mm(v[c], bb, 1, 1)
                    dv = dv + f * mm(k[c], bb, 1, 0)
                dk_ref[0, tok, cols] = dk.astype(BF16)
                dv_ref[0, tok, cols] = dv.astype(BF16)
                if c + 1 < chunks:
                    vf = (f * v[c].astype(F32)).astype(BF16)
                    state = jnp.exp(tot[c]) * state.astype(F32) + mm(k[c], vf, 0, 0)
        for c in range(chunks, nch):
            tok = slice(c * CH, (c + 1) * CH)
            for ref in (out_ref, dq_ref, dk_ref, dv_ref):
                ref[0, tok, :] = jnp.zeros((CH, H * DH), BF16)

    for n in range(1, nch + 1):
        low = (n - 1) * CH
        cond = length > low if n == nch else jnp.logical_and(length > low, length <= n * CH)
        pl.when(cond)(functools.partial(body, n))


def response(lens, adv, q, k, v, cot, rg, mask, starts):
    smem = pl.BlockSpec(memory_space=pltpu.SMEM)
    big = pl.BlockSpec((1, RMAX, H * DH), lambda r: (r, 0, 0))
    shape = jax.ShapeDtypeStruct((NR, RMAX, H * DH), BF16)
    return pl.pallas_call(
        response_kernel,
        grid=(NR,),
        out_shape=(shape,) * 4,
        in_specs=[
            smem,
            smem,
            big,
            big,
            big,
            big,
            pl.BlockSpec((1, H, RMAX), lambda r: (r, 0, 0)),
            pl.BlockSpec((NR, RMAX), lambda r: (0, 0)),
            pl.BlockSpec((1, H * DH, DH), lambda r: (r, 0, 0)),
        ],
        out_specs=(big,) * 4,
        compiler_params=pltpu.CompilerParams(
            dimension_semantics=("arbitrary",), vmem_limit_bytes=48 << 20
        ),
        name="response",
    )(lens, adv, q, k, v, cot, rg, mask, starts)


def shards(pk, pv, pg, q, k, v, rg, cot, gid, lens, mask, adv):
    dk, dv, starts = exchange(gid, lens, adv, pk, pv, pg, q, cot, rg, mask)
    out, dq, rdk, rdv = response(lens, adv, q, k, v, cot, rg, mask, starts)
    return out, dq, rdk, rdv, dk, dv


def solution(mesh):
    both = ("prompt", "resp")
    pieces = P("resp", "prompt", None)
    slots = P(both, None, None)
    return jax.shard_map(
        shards,
        mesh=mesh,
        in_specs=(
            pieces,
            pieces,
            P("resp", None, "prompt"),
            slots,
            slots,
            slots,
            slots,
            slots,
            P(both),
            P(both, None),
            P(both, None),
            P(both),
        ),
        out_specs=(slots, slots, slots, slots, pieces, pieces),
        check_vma=False,
    )
```

time: 525 us -> 56.3 us (0.11)
  waiting for transfers between devices: 392 us -> 0 us
  Pallas kernels: 0 us -> 42.4 us
  local copies, waits for them, and re-layouts: 46.6 us -> 12.7 us
  matrix products: 28 us -> 0 us
  other arithmetic: 19.7 us -> 0 us
  blocking collectives: 17.3 us -> 0 us
  between operations: 14.7 us -> 0.71 us
    psum x2 -> x0, waiting for transfers between devices: 160 us -> none  [the longest x1 80.2 us: from_root(): return lax.psum(jnp.where(mine, x, jnp.zeros_like(x)), axis)]
    reduce_scatter x1 -> x0, waiting for transfers between devices: 127 us -> none  [shards(): owned = lax.psum_scatter(summed, 'resp', scatter_dimension=0, tiled=True)]
    all_gather x2 -> x0, waiting for transfers between devices: 104 us -> none  [the longest x1 84.7 us: shards(): gathered = lax.all_gather(final_state[None], 'resp', axis=0, tiled=True)]
    pallas_call x0 -> x2, Pallas kernels: none -> 42.4 us  [the longest x1 32.9 us: exchange(): pl.pallas_call(exchange_kernel, out_shape=(jax.ShapeDtypeStruct((1, PIECE...]
    dot_general x79 -> x0, matrix products: 28 us -> none  [the longest x8 2.73 us: head_pass(): grad_mix = jnp.dot(grad_out, value_h.T, preferred_element_type=jnp.float32)]
    unnamed x1 -> x0, blocking collectives: 17.3 us -> none
    dynamic_update_slice x32 -> x0, local copies, waits for them, and re-layouts: 13.7 us -> none  [shards(): lax.map(resp_item, (resp_queries, resp_keys, response_value_rows, resp_ga...]
    select_n x11 -> x0, other arithmetic: 9.55 us -> none  [the longest x8 7.96 us: hop(): return jax.tree.map(lambda a, b: jnp.where(reached, a, b), new, before)]
  transfers between devices with their start and end apart: 5 -> 0, of which waited for: 5 -> 0; matrix products, arithmetic and copies ran while one was open for 1% -> 0% of each run, Pallas kernels for 0% -> 0%
where the time goes in v1:
time: 56.3 us; the launch traced here: 55.8 us
  Pallas kernels  42.4 us (75%)
  local copies, waits for them, and re-layouts  12.7 us (23%)
  between operations  0.71 us (1%)
    pallas_call x1, Pallas kernels, exchange(): pl.pallas_call(exchange_kernel, out_shape=(jax.ShapeDtypeStruct((1, PIECE...  32.9 us
    unnamed x36, local copies, waits for them, and re-layouts  12.7 us
    pallas_call x1, Pallas kernels, response(): pl.pallas_call(response_kernel, grid=(NR,), out_shape=(shape,) * 4, in_sp...  9.55 us

profile of v1, /device:TPU:1, one launch (start us, length us, event | category | flops | bytes accessed | tf_op | source)
XLA Modules:
  0.0 55.8 jit_solution(14834903000681650654)
XLA Ops:
  0.6 0.0 copy-start
  0.6 1.2 %copy-done = bf16[4,512,256]{2,1,0:T(8,128)(2,1)S(1)} copy-done((bf16[4,512,256]{2,1,0:T(8,128)(2,1)S(1)}, bf16[4,512,256]{2,1,0:T(8,128)(2,1)}, u32[]{:S(2)}) %copy-start) | copy-done | bytes 1048600
  1.9 1.2 %copy-done.2 = bf16[4,512,256]{2,1,0:T(8,128)(2,1)S(1)} copy-done((bf16[4,512,256]{2,1,0:T(8,128)(2,1)S(1)}, bf16[4,512,256]{2,1,0:T(8,128)(2,1)}, u32[]{:S(2)}) %copy-start.2) | copy-done | bytes 1048600
  3.1 0.9 %copy-done.6 = bf16[1,256,256]{2,1,0:T(8,128)(2,1)S(1)} copy-done((bf16[1,256,256]{2,1,0:T(8,128)(2,1)S(1)}, bf16[1,256,256]{2,1,0:T(8,128)(2,1)}, u32[]{:S(2)}) %copy-start.6) | copy-done | bytes 131096
  4.0 0.9 %copy-done.7 = bf16[1,256,256]{2,1,0:T(8,128)(2,1)S(1)} copy-done((bf16[1,256,256]{2,1,0:T(8,128)(2,1)S(1)}, bf16[1,256,256]{2,1,0:T(8,128)(2,1)}, u32[]{:S(2)}) %copy-start.7) | copy-done | bytes 131096
  4.9 0.7 %copy-done.8 = f32[4,2,512]{2,1,0:T(2,128)S(1)} copy-done((f32[4,2,512]{2,1,0:T(2,128)S(1)}, f32[4,2,512]{2,1,0:T(2,128)}, u32[]{:S(2)}) %copy-start.8) | copy-done | bytes 16408
  5.6 0.7 %copy-done.10 = s32[4,512]{1,0:T(4,128)S(1)} copy-done((s32[4,512]{1,0:T(4,128)S(1)}, s32[4,512]{1,0:T(4,128)}, u32[]{:S(2)}) %copy-start.10) | copy-done | bytes 8216
  6.3 0.7 %copy-done.11 = f32[1,2,256]{2,1,0:T(2,128)S(1)} copy-done((f32[1,2,256]{2,1,0:T(2,128)S(1)}, f32[1,2,256]{2,1,0:T(2,128)}, u32[]{:S(2)}) %copy-start.11) | copy-done | bytes 2072
  7.0 0.7 %copy-done.12 = s32[1,4]{1,0:T(1,128)S(1)} copy-done((s32[1,4]{1,0:T(1,128)S(1)}, s32[1,4]{1,0:T(1,128)}, u32[]{:S(2)}) %copy-start.12) | copy-done | bytes 40
  7.7 0.7 %copy-done.14 = s32[4]{0:T(128)S(1)} copy-done((s32[4]{0:T(128)S(1)}, s32[4]{0:T(128)}, u32[]{:S(2)}) %copy-start.14) | copy-done | bytes 40
  8.3 0.7 %copy-done.16 = s32[4]{0:T(128)S(1)} copy-done((s32[4]{0:T(128)S(1)}, s32[4]{0:T(128)}, u32[]{:S(2)}) %copy-start.16) | copy-done | bytes 40
  9.0 32.9 %exchange.1 = (bf16[1,256,256]{2,1,0:T(8,128)(2,1)S(1)}, bf16[1,256,256]{2,1,0:T(8,128)(2,1)S(1)}, bf16[4,256,128]{2,1,0:T(8,128)(2,1)S(1)}) custom-call(s32[4]{0:T(128)S(1)} %copy-done.16, s32[1,4]{1,0:T(1,128)S(1)} %copy-done.12, s32[4]{0:T(128)S(1)} %copy-done.14, bf16[1,256,256]{2,1,0:T(8,128)(2,1)S(1)} %copy-done.6, bf16[1,256,256]{2,1,0:T(8,128)(2,1)S(1)} %copy-done.7, ...), custom_call_target="tpu_custom_call" | custom-call | tf_op jit(solution)/shard_map/exchange/pallas_call | solution.py:229
  41.8 0.0 copy-start.13
  41.9 0.0 copy-start.15
  41.9 0.0 copy-done.1
  41.9 0.0 copy-done.3
  41.9 0.0 copy-done.9
  41.9 0.6 %copy-done.13 = s32[1,4]{1,0:T(1,128)S(1)} copy-done((s32[1,4]{1,0:T(1,128)S(1)}, s32[1,4]{1,0:T(1,128)}, u32[]{:S(2)}) %copy-start.13) | copy-done | bytes 40
  42.5 0.0 copy-done.15
  42.5 1.2 %copy-done.4 = bf16[4,512,256]{2,1,0:T(8,128)(2,1)S(1)} copy-done((bf16[4,512,256]{2,1,0:T(8,128)(2,1)S(1)}, bf16[4,512,256]{2,1,0:T(8,128)(2,1)}, u32[]{:S(2)}) %copy-start.4) | copy-done | bytes 1048600
  43.8 1.2 %copy-done.5 = bf16[4,512,256]{2,1,0:T(8,128)(2,1)S(1)} copy-done((bf16[4,512,256]{2,1,0:T(8,128)(2,1)S(1)}, bf16[4,512,256]{2,1,0:T(8,128)(2,1)}, u32[]{:S(2)}) %copy-start.5) | copy-done | bytes 1048600
  45.0 9.6 %response.1 = (bf16[4,512,256]{2,1,0:T(8,128)(2,1)}, bf16[4,512,256]{2,1,0:T(8,128)(2,1)}, bf16[4,512,256]{2,1,0:T(8,128)(2,1)}, bf16[4,512,256]{2,1,0:T(8,128)(2,1)}) custom-call(s32[1,4]{1,0:T(1,128)S(1)} %copy-done.13, s32[4]{0:T(128)S(1)} %copy-done.15, bf16[4,512,256]{2,1,0:T(8,128)(2,1)S(1)} %copy-done.1, bf16[4,512,256]{2,1,0:T(8,128)(2,1)S(1)} %copy-done.4, ...), custom_call_target="tpu_custom_call" | custom-call | tf_op jit(solution)/shard_map/response/pallas_call | solution.py:348
  54.5 0.7 %copy.20 = bf16[1,256,256]{2,1,0:T(8,128)(2,1)} copy(bf16[1,256,256]{2,1,0:T(8,128)(2,1)S(1)} %get-tuple-element.30) | data formatting | bytes 262144
  55.2 0.7 %copy.21 = bf16[1,256,256]{2,1,0:T(8,128)(2,1)} copy(bf16[1,256,256]{2,1,0:T(8,128)(2,1)S(1)} %get-tuple-element.31) | data formatting | bytes 262144
  (14 shorter events, 0.0 us)
Async XLA Ops:
  0.6 1.2 %copy-start = (bf16[4,512,256]{2,1,0:T(8,128)(2,1)S(1)}, bf16[4,512,256]{2,1,0:T(8,128)(2,1)}, u32[]{:S(2)}) copy-start(bf16[4,512,256]{2,1,0:T(8,128)(2,1)} %q_ref.1) | copy-start | bytes 3145732
  1.9 1.2 %copy-start.2 = (bf16[4,512,256]{2,1,0:T(8,128)(2,1)S(1)}, bf16[4,512,256]{2,1,0:T(8,128)(2,1)}, u32[]{:S(2)}) copy-start(bf16[4,512,256]{2,1,0:T(8,128)(2,1)} %cot_ref.1) | copy-start | bytes 3145732
  3.1 0.9 %copy-start.6 = (bf16[1,256,256]{2,1,0:T(8,128)(2,1)S(1)}, bf16[1,256,256]{2,1,0:T(8,128)(2,1)}, u32[]{:S(2)}) copy-start(bf16[1,256,256]{2,1,0:T(8,128)(2,1)} %pk_hbm.1) | copy-start | bytes 393220
  4.0 0.9 %copy-start.7 = (bf16[1,256,256]{2,1,0:T(8,128)(2,1)S(1)}, bf16[1,256,256]{2,1,0:T(8,128)(2,1)}, u32[]{:S(2)}) copy-start(bf16[1,256,256]{2,1,0:T(8,128)(2,1)} %pv_hbm.1) | copy-start | bytes 393220
  4.9 0.7 %copy-start.8 = (f32[4,2,512]{2,1,0:T(2,128)S(1)}, f32[4,2,512]{2,1,0:T(2,128)}, u32[]{:S(2)}) copy-start(f32[4,2,512]{2,1,0:T(2,128)} %rg.3) | copy-start | bytes 49156
  5.6 0.7 %copy-start.10 = (s32[4,512]{1,0:T(4,128)S(1)}, s32[4,512]{1,0:T(4,128)}, u32[]{:S(2)}) copy-start(s32[4,512]{1,0:T(4,128)} %mask.3) | copy-start | bytes 24580
  6.3 0.7 %copy-start.11 = (f32[1,2,256]{2,1,0:T(2,128)S(1)}, f32[1,2,256]{2,1,0:T(2,128)}, u32[]{:S(2)}) copy-start(f32[1,2,256]{2,1,0:T(2,128)} %pg.1) | copy-start | bytes 6148
  7.0 0.7 %copy-start.12 = (s32[1,4]{1,0:T(1,128)S(1)}, s32[1,4]{1,0:T(1,128)}, u32[]{:S(2)}) copy-start(s32[1,4]{1,0:T(1,128)} %lens.3) | copy-start | bytes 52
  7.6 0.7 %copy-start.14 = (s32[4]{0:T(128)S(1)}, s32[4]{0:T(128)}, u32[]{:S(2)}) copy-start(s32[4]{0:T(128)} %adv.3) | copy-start | bytes 52
  8.3 0.7 %copy-start.16 = (s32[4]{0:T(128)S(1)}, s32[4]{0:T(128)}, u32[]{:S(2)}) copy-start(s32[4]{0:T(128)} %gid.1) | copy-start | bytes 52
  9.0 32.9 %copy-start.1 = (bf16[4,512,256]{2,1,0:T(8,128)(2,1)S(1)}, bf16[4,512,256]{2,1,0:T(8,128)(2,1)}, u32[]{:S(2)}) copy-start(bf16[4,512,256]{2,1,0:T(8,128)(2,1)} %q_ref.1) | copy-start | bytes 3145732
  9.0 32.9 %copy-start.3 = (bf16[4,512,256]{2,1,0:T(8,128)(2,1)S(1)}, bf16[4,512,256]{2,1,0:T(8,128)(2,1)}, u32[]{:S(2)}) copy-start(bf16[4,512,256]{2,1,0:T(8,128)(2,1)} %cot_ref.1) | copy-start | bytes 3145732
  9.0 32.9 %copy-start.9 = (f32[4,2,512]{2,1,0:T(2,128)S(1)}, f32[4,2,512]{2,1,0:T(2,128)}, u32[]{:S(2)}) copy-start(f32[4,2,512]{2,1,0:T(2,128)} %rg.3) | copy-start | bytes 49156
  41.8 0.7 %copy-start.13 = (s32[1,4]{1,0:T(1,128)S(1)}, s32[1,4]{1,0:T(1,128)}, u32[]{:S(2)}) copy-start(s32[1,4]{1,0:T(1,128)} %lens.3) | copy-start | bytes 52
  41.9 0.7 %copy-start.15 = (s32[4]{0:T(128)S(1)}, s32[4]{0:T(128)}, u32[]{:S(2)}) copy-start(s32[4]{0:T(128)} %adv.3) | copy-start | bytes 52
  42.5 1.2 %copy-start.4 = (bf16[4,512,256]{2,1,0:T(8,128)(2,1)S(1)}, bf16[4,512,256]{2,1,0:T(8,128)(2,1)}, u32[]{:S(2)}) copy-start(bf16[4,512,256]{2,1,0:T(8,128)(2,1)} %k_ref.1) | copy-start | bytes 3145732
  43.7 1.2 %copy-start.5 = (bf16[4,512,256]{2,1,0:T(8,128)(2,1)S(1)}, bf16[4,512,256]{2,1,0:T(8,128)(2,1)}, u32[]{:S(2)}) copy-start(bf16[4,512,256]{2,1,0:T(8,128)(2,1)} %v_ref.1) | copy-start | bytes 3145732

commit v2 on v1

v2 whole, which is shorter than its diff:
```python
import jax
import jax.numpy as jnp
from jax import lax
from jax.experimental import pallas as pl
from jax.experimental.pallas import tpu as pltpu
from jax.sharding import PartitionSpec as P

H = 2
DH = 128
RMAX = 512
NR = 4
PIECE = 256
PLANE = 32
RING = 8
CH = 256
HI = lax.Precision.HIGHEST
MESH = pl.DeviceIdType.MESH
F32 = jnp.float32
BF16 = jnp.bfloat16
HEADS = [slice(h * DH, (h + 1) * DH) for h in range(H)]
TOKENS = [slice(c * CH, (c + 1) * CH) for c in range(RMAX // CH)]


def mm(x, y, cx, cy, **kw):
    return lax.dot_general(x, y, (((cx,), (cy,)), ((), ())), preferred_element_type=F32, **kw)


def split(x):
    hi = x.astype(BF16)
    return hi, (x - hi.astype(F32)).astype(BF16)


def iota(shape, axis):
    return lax.broadcasted_iota(jnp.int32, shape, axis)


def col(cols, r, item):
    return cols[:, r * 16 + item : r * 16 + item + 1]


def exchange_kernel(
    gid_hbm, lens_hbm, adv_hbm, pk_hbm, pv_hbm, pg_hbm, q_hbm, k_hbm, v_hbm, cot_hbm, rg_hbm, mask_hbm,
    pk, pv, q, go, pout, pdq, dk, dv, starts, gfin, cols_out, pfac,
    gid, lens, adv, pg, k, v, rg, mask, crows, cfull, back,
    f1s, f1r, ids, idr, f2s, f2r, f3s, f3r, g1s, g1r, g2s, g2r, g3s, g3r, oh,
    in_sems, send_sems, recv_sems,
):
    a = lax.axis_index("prompt")
    b = lax.axis_index("resp")
    quad = lax.div(b, 16) * 2 + lax.rem(b, 2)
    z = lax.rem(lax.div(b, 2), RING)
    me = a * 4 + quad
    quads = [lax.rem(quad + d, 4) for d in range(4)]
    homes = [lax.div(x, 2) * 16 + z * 2 + lax.rem(x, 2) for x in quads]
    corner = lax.div(b, 16) * 16 + lax.rem(b, 2)
    rings = [lax.rem(z + d, RING) for d in (4, 3, 5, 2, 6, 1, 7)]

    loads = [
        pltpu.make_async_copy(s, d, in_sems.at[i])
        for i, (s, d) in enumerate(
            (
                (pg_hbm, pg), (pk_hbm, pk), (pv_hbm, pv), (gid_hbm, gid), (lens_hbm, lens), (adv_hbm, adv),
                (rg_hbm, rg), (mask_hbm, mask), (cot_hbm, go), (q_hbm, q), (k_hbm, k), (v_hbm, v),
            )
        )
    ]
    for c in loads:
        c.start()

    def to_plane(fn):
        def others(d, _):
            aa = lax.rem(a + d, 8)
            for x, home in zip(quads, homes):
                fn(aa * 4 + x, (aa, home))
            return 0

        lax.fori_loop(1, 8, others, 0)
        for d in (3, 2, 1):
            fn(a * 4 + quads[d], (a, homes[d]))

    def to_ring(fn):
        for zz in rings:
            fn(zz, (a, corner + zz * 2))

    barrier = pltpu.get_barrier_semaphore()

    def greet(_, dev):
        pl.semaphore_signal(barrier, inc=1, device_id=dev, device_id_type=MESH)

    to_plane(greet)
    to_ring(greet)

    def send(stage, src_of, dst):
        def one(j, dev):
            pltpu.make_async_remote_copy(
                src_ref=src_of(j),
                dst_ref=dst,
                send_sem=send_sems.at[stage],
                recv_sem=recv_sems.at[stage],
                device_id=dev,
                device_id_type=MESH,
            ).start()

        return one

    def wait_all(ref, sems, stage):
        pltpu.make_async_copy(ref, ref, sems.at[stage]).wait()

    for c in loads[:6]:
        c.wait()
    gates = jnp.concatenate([pg[0], jnp.zeros((6, PIECE), F32)], axis=0)
    later = (iota((PIECE, PIECE), 1) > iota((PIECE, PIECE), 0)).astype(F32)
    suf = mm(later, gates, 1, 1, precision=HI)
    total = jnp.sum(gates, axis=1, keepdims=True)
    esuf = jnp.exp(suf)
    for h in range(H):
        hi, lo = split(esuf[:, h : h + 1] * pv[0, :, HEADS[h]].astype(F32))
        kh = pk[0, :, HEADS[h]]
        state = mm(kh, hi, 0, 0) + mm(kh, lo, 0, 0)
        f1s[h * 16 : (h + 1) * 16] = state.reshape(16, 8, DH)
    row = iota((8, DH), 0)
    meta = jnp.broadcast_to(total, (8, DH))
    for r in range(NR):
        g = gid[r]
        slot = ((g >> 1) & 7) * 4 + (g >> 4) * 2 + (g & 1)
        meta = jnp.where(row == 2 + r, (slot * 8).astype(F32), meta)
    ids[...] = meta
    f1r[me] = f1s[me]
    idr[me] = meta

    for c in loads[6:8]:
        c.wait()
    upper = (iota((CH, CH), 0) <= iota((CH, CH), 1)).astype(F32)
    lane = iota((1, CH), 1)
    grows = jnp.concatenate([rg[r, :, t] for r in range(NR) for t in TOKENS], axis=0)
    cums = mm(grows, upper, 1, 0, precision=HI)
    crows[...] = cums
    exps = jnp.exp(cums)
    tots = cums[:, CH - 1 : CH]
    falls = jnp.exp(tots - cums)
    rows = []
    for r in range(NR):
        rows += [cums[4 * r : 4 * r + 4], exps[4 * r : 4 * r + 4]]
        opens = [jnp.where(lane + c * CH < lens[0, r], 1.0, 0.0) for c in range(len(TOKENS))]
        for on, t in zip(opens, TOKENS):
            rows.append(on * mask[r : r + 1, t].astype(F32) * (adv[r].astype(F32) * (1.0 / 1024.0)))
        rows += [falls[4 * r : 4 * r + 2]] + opens + [jnp.zeros((2, CH), F32)]
    cols = jnp.concatenate(rows + [jnp.zeros((64, CH), F32)], axis=0).T
    cols_out[...] = cols
    for c in loads[8:10]:
        c.wait()
    for pair in range(NR // 2):
        for h in range(H):
            found = []
            for r in (2 * pair, 2 * pair + 1):
                parts = []
                for c, t in enumerate(TOKENS):
                    grad_out = (go[r, t, HEADS[h]].astype(F32) * col(cols, r, 8 + c)).astype(BF16)
                    go[r, t, HEADS[h]] = grad_out
                    scaled = (grad_out.astype(F32) * col(cols, r, 4 + 2 * c + h)).astype(BF16)
                    parts.append(mm(q[r, t, HEADS[h]], scaled, 0, 0))
                back[r, h] = parts[1].astype(BF16)
                fall = jnp.exp(tots[4 * r + h : 4 * r + h + 1])
                found.append((parts[0] + fall * parts[1]).reshape(16, 8, DH))
            g1s[h * 16 : (h + 1) * 16, pair * 16 : (pair + 1) * 16, :] = jnp.concatenate(
                found, axis=1
            ).astype(BF16)
    g1r[me] = g1s[me]

    pl.semaphore_wait(barrier, PLANE - 1 + RING - 1)
    to_plane(send(0, lambda j: f1s.at[j], f1r.at[me]))
    to_plane(send(6, lambda j: ids, idr.at[me]))
    to_plane(send(3, lambda j: g1s.at[j], g1r.at[me]))

    loads[10].wait()
    loads[11].wait()
    causal = iota((CH, CH), 0) >= iota((CH, CH), 1)

    def inner(r):
        for h in range(H):
            hs = HEADS[h]
            bk = back[r, h]
            step = None
            for c, t in enumerate(TOKENS):
                qc, kc, vc, gc = q[r, t, hs], k[r, t, hs], v[r, t, hs], go[r, t, hs]
                i = 4 * r + 2 * c + h
                decay = jnp.exp(jnp.where(causal, col(cols, r, 2 * c + h) - crows[i : i + 1, :], -1e30))
                mix = (mm(qc, kc, 1, 1) * decay).astype(BF16)
                gs = (mm(gc, vc, 1, 1) * decay).astype(BF16)
                out = mm(mix, vc, 1, 0)
                dq = mm(gs, kc, 1, 0)
                dkc = mm(gs, qc, 0, 0)
                dvc = mm(mix, gc, 0, 0)
                if c == 0:
                    f = col(cols, r, 10 + h)
                    dkc = dkc + f * mm(vc, bk, 1, 1)
                    dvc = dvc + f * mm(kc, bk, 1, 0)
                    step = mm(kc, (f * vc.astype(F32)).astype(BF16), 0, 0).astype(BF16)
                else:
                    e = col(cols, r, 4 + 2 * c + h)
                    out = out + e * mm(qc, step, 1, 0)
                    dq = dq + e * mm(gc, step, 1, 1)
                pout[r, t, hs] = out
                pdq[r, t, hs] = dq
                dk[r, t, hs] = dkc.astype(BF16)
                dv[r, t, hs] = dvc.astype(BF16)

    inner(0)
    inner(1)
    inner(2)

    wait_all(f1r.at[pl.ds(0, PLANE - 1)], recv_sems, 0)
    wait_all(idr.at[pl.ds(0, PLANE - 1)], recv_sems, 6)
    data = f1r[...].reshape(8, 4, 8, DH)
    logs = jnp.where(a >= 4, idr[:, 1:2, :], idr[:, 0:1, :]).reshape(8, 4, 1, DH)
    acc = data[7]
    run = logs[7]
    for piece in range(6, -1, -1):
        acc = acc + jnp.exp(run) * data[piece]
        run = run + logs[piece]
    f2s[...] = acc.reshape(32, DH).astype(BF16)
    f2r[z] = f2s[...]
    to_ring(send(1, lambda j: f2s, f2r.at[z]))

    sub = iota((1, 8, DH), 1).astype(F32)
    wide = jnp.concatenate(
        [jnp.broadcast_to(idr[:, 2 + r : 3 + r, :], (PLANE, 8, DH)) + sub for r in range(NR)], axis=1
    ).reshape(PLANE * 32, DH)
    lanes = iota((1, DH), 1).astype(F32)
    oh[:, 0:DH] = jnp.where(wide == lanes, 1.0, 0.0).astype(BF16)
    oh[:, DH : 2 * DH] = jnp.where(wide == lanes + float(DH), 1.0, 0.0).astype(BF16)

    wait_all(g1r.at[pl.ds(0, PLANE - 1)], recv_sems, 3)
    added = mm(oh[...], g1r[...].reshape(PLANE * 32, DH), 0, 0)
    g2s[...] = added.astype(BF16).reshape(RING, 32, DH)
    g2r[z] = g2s[z]
    to_ring(send(4, lambda j: g2s.at[j], g2r.at[z]))

    wait_all(f2r.at[pl.ds(0, RING - 1)], recv_sems, 1)
    picked = mm(oh[...], f2r[...].reshape(RING * 32, DH), 1, 0)
    f3s[...] = picked.astype(BF16).reshape(PLANE, 32, DH)
    f3r[me] = f3s[me]
    to_plane(send(2, lambda j: f3s.at[j], f3r.at[me]))

    after = jnp.zeros((8, DH), F32)
    for piece in range(8):
        after = after + jnp.where(piece > a, idr[piece * 4 + quad], 0.0)
    lane8 = iota((PIECE, 8), 1)
    pfac[:, 0:8] = jnp.exp(suf + jnp.where(lane8 == 0, after[0:1, 0:1], after[1:2, 0:1]))

    wait_all(g2r.at[pl.ds(0, RING - 1)], recv_sems, 4)
    g3s[...] = jnp.sum(g2r[...].astype(F32), axis=0).reshape(4, 8, DH)
    g3r[me] = g3s[quad]
    to_plane(send(5, lambda j: g3s.at[lax.rem(j, 4)], g3r.at[me]))

    inner(3)

    wait_all(g3r.at[pl.ds(0, PLANE - 1)], recv_sems, 5)
    gfin[...] = g3r[...].reshape(H * DH, DH)

    wait_all(f3r.at[pl.ds(0, PLANE - 1)], recv_sems, 2)
    got = f3r[...].astype(F32)
    for r in range(NR):
        starts[r] = got[:, r * 8 : (r + 1) * 8, :].reshape(2 * DH, DH).astype(BF16)

    wait_all(f1s.at[pl.ds(0, PLANE - 1)], send_sems, 0)
    wait_all(f2r.at[pl.ds(0, RING - 1)], send_sems, 1)
    wait_all(f3s.at[pl.ds(0, PLANE - 1)], send_sems, 2)
    wait_all(g1s.at[pl.ds(0, PLANE - 1)], send_sems, 3)
    wait_all(g2s.at[pl.ds(0, RING - 1)], send_sems, 4)
    wait_all(g3r.at[pl.ds(0, PLANE - 1)], send_sems, 5)
    wait_all(idr.at[pl.ds(0, PLANE - 1)], send_sems, 6)


def exchange(*args):
    hbm = pl.BlockSpec(memory_space=pltpu.HBM)
    vmem = pl.BlockSpec(memory_space=pltpu.VMEM)
    shapes = (
        ((1, PIECE, H * DH), BF16),
        ((1, PIECE, H * DH), BF16),
        ((NR, RMAX, H * DH), BF16),
        ((NR, RMAX, H * DH), BF16),
        ((NR, RMAX, H * DH), F32),
        ((NR, RMAX, H * DH), F32),
        ((NR, RMAX, H * DH), BF16),
        ((NR, RMAX, H * DH), BF16),
        ((NR, H * DH, DH), BF16),
        ((H * DH, DH), F32),
        ((CH, DH), F32),
        ((PIECE, DH), F32),
    )
    return pl.pallas_call(
        exchange_kernel,
        out_shape=tuple(pltpu.VMEM(s, t) for s, t in shapes),
        in_specs=[hbm] * 12,
        out_specs=(vmem,) * 12,
        scratch_shapes=[
            pltpu.SMEM((NR,), jnp.int32),
            pltpu.SMEM((1, NR), jnp.int32),
            pltpu.SMEM((NR,), jnp.int32),
            pltpu.VMEM((1, H, PIECE), F32),
            pltpu.VMEM((NR, RMAX, H * DH), BF16),
            pltpu.VMEM((NR, RMAX, H * DH), BF16),
            pltpu.VMEM((NR, H, RMAX), F32),
            pltpu.VMEM((NR, RMAX), jnp.int32),
            pltpu.VMEM((NR * 4, CH), F32),
            pltpu.VMEM((8, DH), F32),
            pltpu.VMEM((NR, H, DH, DH), BF16),
            pltpu.VMEM((PLANE, 8, DH), F32),
            pltpu.VMEM((PLANE, 8, DH), F32),
            pltpu.VMEM((8, DH), F32),
            pltpu.VMEM((PLANE, 8, DH), F32),
            pltpu.VMEM((32, DH), BF16),
            pltpu.VMEM((RING, 32, DH), BF16),
            pltpu.VMEM((PLANE, 32, DH), BF16),
            pltpu.VMEM((PLANE, 32, DH), BF16),
            pltpu.VMEM((PLANE, 32, DH), BF16),
            pltpu.VMEM((PLANE, 32, DH), BF16),
            pltpu.VMEM((RING, 32, DH), BF16),
            pltpu.VMEM((RING, 32, DH), BF16),
            pltpu.VMEM((4, 8, DH), F32),
            pltpu.VMEM((PLANE, 8, DH), F32),
            pltpu.VMEM((PLANE * 32, 2 * DH), BF16),
            pltpu.SemaphoreType.DMA((12,)),
            pltpu.SemaphoreType.DMA((7,)),
            pltpu.SemaphoreType.DMA((7,)),
        ],
        compiler_params=pltpu.CompilerParams(
            collective_id=0, has_side_effects=True, vmem_limit_bytes=32 << 20
        ),
        name="exchange",
    )(*args)


def finish_kernel(
    pk, pv, q, go, pout, pdq, dk, dv, starts, gfin, cols_ref, pfac,
    out_hbm, dq_hbm, dk_hbm, dv_hbm, pdk_hbm, pdv_hbm, out, dq, pdk, pdv, sems,
):
    early = [
        pltpu.make_async_copy(dk, dk_hbm, sems.at[0]),
        pltpu.make_async_copy(dv, dv_hbm, sems.at[1]),
    ]
    for c in early:
        c.start()
    cols = cols_ref[...]
    for r in range(NR):
        for h in range(H):
            hs = HEADS[h]
            state = starts[r, hs, :]
            span = None
            for c, t in enumerate(TOKENS):
                e = col(cols, r, 4 + 2 * c + h)
                if c == 1:
                    e = e * span
                span = e[CH - 1 : CH]
                o = pout[r, t, hs] + e * mm(q[r, t, hs], state, 1, 0)
                out[r, t, hs] = (o * col(cols, r, 12 + c)).astype(BF16)
                dq[r, t, hs] = (pdq[r, t, hs] + e * mm(go[r, t, hs], state, 1, 1)).astype(BF16)
        for i, (s, d) in enumerate(((out, out_hbm), (dq, dq_hbm))):
            c = pltpu.make_async_copy(s.at[r], d.at[r], sems.at[2 + 2 * r + i])
            c.start()
            early.append(c)
    for h in range(H):
        hs = HEADS[h]
        factor = pfac[:, h : h + 1]
        hi, lo = split(gfin[hs, :])
        vh, kh = pv[0, :, hs], pk[0, :, hs]
        pdk[0, :, hs] = (factor * (mm(vh, hi, 1, 1) + mm(vh, lo, 1, 1))).astype(BF16)
        pdv[0, :, hs] = (factor * (mm(kh, hi, 1, 0) + mm(kh, lo, 1, 0))).astype(BF16)
    for i, (s, d) in enumerate(((pdk, pdk_hbm), (pdv, pdv_hbm))):
        c = pltpu.make_async_copy(s, d, sems.at[10 + i])
        c.start()
        early.append(c)
    for c in early:
        c.wait()


def finish(*parts):
    vmem = pl.BlockSpec(memory_space=pltpu.VMEM)
    hbm = pl.BlockSpec(memory_space=pltpu.HBM)
    big = jax.ShapeDtypeStruct((NR, RMAX, H * DH), BF16)
    small = jax.ShapeDtypeStruct((1, PIECE, H * DH), BF16)
    return pl.pallas_call(
        finish_kernel,
        out_shape=(big,) * 4 + (small,) * 2,
        in_specs=[vmem] * 12,
        out_specs=(hbm,) * 6,
        scratch_shapes=[
            pltpu.VMEM((NR, RMAX, H * DH), BF16),
            pltpu.VMEM((NR, RMAX, H * DH), BF16),
            pltpu.VMEM((1, PIECE, H * DH), BF16),
            pltpu.VMEM((1, PIECE, H * DH), BF16),
            pltpu.SemaphoreType.DMA((12,)),
        ],
        compiler_params=pltpu.CompilerParams(vmem_limit_bytes=24 << 20),
        name="finish",
    )(*parts)


def shards(pk, pv, pg, q, k, v, rg, cot, gid, lens, mask, adv):
    parts = exchange(*[pltpu.with_memory_space_constraint(x, pltpu.HBM) for x in (gid, lens, adv, pk, pv, pg, q, k, v, cot, rg, mask)])
    return finish(*parts)


def solution(mesh):
    both = ("prompt", "resp")
    pieces = P("resp", "prompt", None)
    slots = P(both, None, None)
    return jax.shard_map(
        shards,
        mesh=mesh,
        in_specs=(
            pieces,
            pieces,
            P("resp", None, "prompt"),
            slots,
            slots,
            slots,
            slots,
            slots,
            P(both),
            P(both, None),
            P(both, None),
            P(both),
        ),
        out_specs=(slots, slots, slots, slots, pieces, pieces),
        check_vma=False,
    )
```

time: 56.3 us -> 33.8 us (0.60)
  local copies, waits for them, and re-layouts: 12.7 us -> 0 us
  Pallas kernels: 42.4 us -> 33.1 us
    unnamed x36 -> x0, local copies, waits for them, and re-layouts: 12.7 us -> none
    pallas_call x2, Pallas kernels: 42.4 us -> 33.1 us  [the longest x1 30.9 us: exchange(): pl.pallas_call(exchange_kernel, out_shape=tuple((pltpu.VMEM(s, t) for s,...]
where the time goes in v2:
time: 33.8 us
  Pallas kernels  33.1 us (98%)
  between operations  0.64 us (2%)
    pallas_call x1, Pallas kernels, exchange(): pl.pallas_call(exchange_kernel, out_shape=tuple((pltpu.VMEM(s, t) for s,...  30.9 us
    pallas_call x1, Pallas kernels, finish(): pl.pallas_call(finish_kernel, out_shape=(big,) * 4 + (small,) * 2, in_spe...  2.18 us

profile of v2, /device:TPU:1, one launch (start us, length us, event | category | flops | bytes accessed | tf_op | source)
XLA Modules:
  0.0 33.8 jit_solution(14081798165578555005)
XLA Ops:
  0.6 30.9 %exchange.1 = (bf16[1,256,256]{2,1,0:T(8,128)(2,1)S(1)}, bf16[1,256,256]{2,1,0:T(8,128)(2,1)S(1)}, bf16[4,512,256]{2,1,0:T(8,128)(2,1)S(1)}, bf16[4,512,256]{2,1...) custom-call(s32[4]{0:T(128)} %gid_hbm.1, ...), custom_call_target="tpu_custom_call" | custom-call | tf_op jit(solution)/shard_map/exchange/pallas_call | solution.py:292
  31.6 2.2 %finish.1 = (bf16[4,512,256]{2,1,0:T(8,128)(2,1)}, bf16[4,512,256]{2,1,0:T(8,128)(2,1)}, bf16[4,512,256]{2,1,0:T(8,128)(2,1)}, bf16[4,512,256]{2,1,0:T(8,128)(2,...) custom-call(bf16[1,256,256]{2,1,0:T(8,128)(2,1)S(1)} %get-tuple-element.18.pk, ...), custom_call_target="tpu_custom_call" | custom-call | tf_op jit(solution)/shard_map/finish/pallas_call | solution.py:383

commit v3 on v2

--- a/solution.py
+++ b/solution.py
@@ -41,8 +41,8 @@
 def exchange_kernel(
     gid_hbm, lens_hbm, adv_hbm, pk_hbm, pv_hbm, pg_hbm, q_hbm, k_hbm, v_hbm, cot_hbm, rg_hbm, mask_hbm,
     pk, pv, q, go, pout, pdq, dk, dv, starts, gfin, cols_out, pfac,
-    gid, lens, adv, pg, k, v, rg, mask, crows, cfull, back,
-    f1s, f1r, ids, idr, f2s, f2r, f3s, f3r, g1s, g1r, g2s, g2r, g3s, g3r, oh,
+    gid, lens, adv, pg, k, v, rg, mask, crows, back,
+    f1s, f1r, ids, idr, f2s, f2r, f3s, f3r, g1s, g1r, g2s, g2r, g3s, g3r, oh, oht,
     in_sems, send_sems, recv_sems,
 ):
     a = lax.axis_index("prompt")
@@ -50,8 +50,23 @@
     quad = lax.div(b, 16) * 2 + lax.rem(b, 2)
     z = lax.rem(lax.div(b, 2), RING)
     me = a * 4 + quad
-    quads = [lax.rem(quad + d, 4) for d in range(4)]
-    homes = [lax.div(x, 2) * 16 + z * 2 + lax.rem(x, 2) for x in quads]
+    near, core = lax.div(b, 16), lax.rem(b, 2)
+    columns = {
+        (fx, dy): lax.rem(lax.div(a, 4) + fx, 2) * 4 + lax.rem(lax.rem(a, 4) + dy, 4)
+        for fx in range(2)
+        for dy in range(4)
+    }
+    quads, homes = {}, {}
+    for fh in range(2):
+        for fc in range(2):
+            hi, lo = lax.rem(near + fh, 2), lax.rem(core + fc, 2)
+            quads[fh, fc] = hi * 2 + lo
+            homes[fh, fc] = hi * 16 + z * 2 + lo
+    order = sorted(
+        ((fx, dy, fh, fc) for fx in range(2) for dy in range(4) for fh in range(2) for fc in range(2)),
+        key=lambda p: -((1 if p[0] else 2 * p[2]) + (0, 1, 2, 1)[p[1]]) * 2 - p[3],
+    )
+    order.remove((0, 0, 0, 0))
     corner = lax.div(b, 16) * 16 + lax.rem(b, 2)
     rings = [lax.rem(z + d, RING) for d in (4, 3, 5, 2, 6, 1, 7)]
 
@@ -59,8 +74,8 @@
         pltpu.make_async_copy(s, d, in_sems.at[i])
         for i, (s, d) in enumerate(
             (
-                (pg_hbm, pg), (pk_hbm, pk), (pv_hbm, pv), (gid_hbm, gid), (lens_hbm, lens), (adv_hbm, adv),
-                (rg_hbm, rg), (mask_hbm, mask), (cot_hbm, go), (q_hbm, q), (k_hbm, k), (v_hbm, v),
+                (pg_hbm, pg), (rg_hbm, rg), (lens_hbm, lens), (adv_hbm, adv), (mask_hbm, mask), (gid_hbm, gid),
+                (pk_hbm, pk), (pv_hbm, pv), (cot_hbm, go), (q_hbm, q), (k_hbm, k), (v_hbm, v),
             )
         )
     ]
@@ -68,15 +83,9 @@
         c.start()
 
     def to_plane(fn):
-        def others(d, _):
-            aa = lax.rem(a + d, 8)
-            for x, home in zip(quads, homes):
-                fn(aa * 4 + x, (aa, home))
-            return 0
-
-        lax.fori_loop(1, 8, others, 0)
-        for d in (3, 2, 1):
-            fn(a * 4 + quads[d], (a, homes[d]))
+        for fx, dy, fh, fc in order:
+            aa = columns[fx, dy]
+            fn(aa * 4 + quads[fh, fc], (aa, homes[fh, fc]))
 
     def to_ring(fn):
         for zz in rings:
@@ -106,35 +115,13 @@
     def wait_all(ref, sems, stage):
         pltpu.make_async_copy(ref, ref, sems.at[stage]).wait()
 
-    for c in loads[:6]:
-        c.wait()
-    gates = jnp.concatenate([pg[0], jnp.zeros((6, PIECE), F32)], axis=0)
-    later = (iota((PIECE, PIECE), 1) > iota((PIECE, PIECE), 0)).astype(F32)
-    suf = mm(later, gates, 1, 1, precision=HI)
-    total = jnp.sum(gates, axis=1, keepdims=True)
-    esuf = jnp.exp(suf)
-    for h in range(H):
-        hi, lo = split(esuf[:, h : h + 1] * pv[0, :, HEADS[h]].astype(F32))
-        kh = pk[0, :, HEADS[h]]
-        state = mm(kh, hi, 0, 0) + mm(kh, lo, 0, 0)
-        f1s[h * 16 : (h + 1) * 16] = state.reshape(16, 8, DH)
-    row = iota((8, DH), 0)
-    meta = jnp.broadcast_to(total, (8, DH))
-    for r in range(NR):
-        g = gid[r]
-        slot = ((g >> 1) & 7) * 4 + (g >> 4) * 2 + (g & 1)
-        meta = jnp.where(row == 2 + r, (slot * 8).astype(F32), meta)
-    ids[...] = meta
-    f1r[me] = f1s[me]
-    idr[me] = meta
-
-    for c in loads[6:8]:
+    for c in loads[:5]:
         c.wait()
     upper = (iota((CH, CH), 0) <= iota((CH, CH), 1)).astype(F32)
     lane = iota((1, CH), 1)
-    grows = jnp.concatenate([rg[r, :, t] for r in range(NR) for t in TOKENS], axis=0)
+    grows = jnp.concatenate([rg[r, :, t] for r in range(NR) for t in TOKENS] + [pg[0]], axis=0)
     cums = mm(grows, upper, 1, 0, precision=HI)
-    crows[...] = cums
+    crows[...] = cums[: NR * 4]
     exps = jnp.exp(cums)
     tots = cums[:, CH - 1 : CH]
     falls = jnp.exp(tots - cums)
@@ -145,8 +132,29 @@
         for on, t in zip(opens, TOKENS):
             rows.append(on * mask[r : r + 1, t].astype(F32) * (adv[r].astype(F32) * (1.0 / 1024.0)))
         rows += [falls[4 * r : 4 * r + 2]] + opens + [jnp.zeros((2, CH), F32)]
-    cols = jnp.concatenate(rows + [jnp.zeros((64, CH), F32)], axis=0).T
+    rows += [falls[NR * 4 : NR * 4 + 2], jnp.zeros((62, CH), F32)]
+    cols = jnp.concatenate(rows, axis=0).T
     cols_out[...] = cols
+
+    for c in loads[5:8]:
+        c.wait()
+    for h in range(H):
+        hi, lo = split(cols[:, 64 + h : 65 + h] * pv[0, :, HEADS[h]].astype(F32))
+        kh = pk[0, :, HEADS[h]]
+        state = mm(kh, hi, 0, 0) + mm(kh, lo, 0, 0)
+        f1s[h * 16 : (h + 1) * 16] = state.reshape(16, 8, DH).astype(BF16)
+    lane = iota((1, DH), 1)
+    meta = jnp.zeros((1, DH), F32)
+    for h in range(H):
+        meta = jnp.where(lane == h, tots[NR * 4 + h : NR * 4 + h + 1], meta)
+    for r in range(NR):
+        g = gid[r]
+        slot = ((g >> 1) & 7) * 4 + (g >> 4) * 2 + (g & 1)
+        meta = jnp.where(lane == 2 + r, (slot * 8).astype(F32), meta)
+    ids[...] = meta
+    f1r[me] = f1s[me]
+    idr[me] = meta
+
     for c in loads[8:10]:
         c.wait()
     for pair in range(NR // 2):
@@ -168,8 +176,8 @@
     g1r[me] = g1s[me]
 
     pl.semaphore_wait(barrier, PLANE - 1 + RING - 1)
+    to_plane(send(6, lambda j: ids, idr.at[me]))
     to_plane(send(0, lambda j: f1s.at[j], f1r.at[me]))
-    to_plane(send(6, lambda j: ids, idr.at[me]))
     to_plane(send(3, lambda j: g1s.at[j], g1r.at[me]))
 
     loads[10].wait()
@@ -207,31 +215,38 @@
 
     inner(0)
     inner(1)
-    inner(2)
+
+    wait_all(idr.at[pl.ds(0, PLANE - 1)], recv_sems, 6)
+    sub = iota((1, 8, DH), 1).astype(F32)
+    wide = jnp.concatenate(
+        [jnp.broadcast_to(idr[:, :, 2 + r : 3 + r], (PLANE, 8, DH)) + sub for r in range(NR)], axis=1
+    ).reshape(PLANE * 32, DH)
+    lanes = iota((1, DH), 1).astype(F32)
+    picks = [jnp.where(wide == lanes + float(i * DH), 1.0, 0.0).astype(BF16) for i in range(2)]
+    for i in range(2):
+        oh[:, i * DH : (i + 1) * DH] = picks[i]
+        oht[i * DH : (i + 1) * DH, :] = picks[i].T
+    logs = idr[...].reshape(8, 4, 1, DH)
+    run = logs[7]
+    keeps = []
+    for piece in range(6, -1, -1):
+        keep = jnp.exp(run)
+        keeps.append(jnp.where(a >= 4, keep[:, :, 1:2], keep[:, :, 0:1]))
+        run = run + logs[piece]
 
     wait_all(f1r.at[pl.ds(0, PLANE - 1)], recv_sems, 0)
-    wait_all(idr.at[pl.ds(0, PLANE - 1)], recv_sems, 6)
-    data = f1r[...].reshape(8, 4, 8, DH)
-    logs = jnp.where(a >= 4, idr[:, 1:2, :], idr[:, 0:1, :]).reshape(8, 4, 1, DH)
+    data = f1r[...].astype(F32).reshape(8, 4, 8, DH)
     acc = data[7]
-    run = logs[7]
     for piece in range(6, -1, -1):
-        acc = acc + jnp.exp(run) * data[piece]
-        run = run + logs[piece]
+        acc = acc + keeps[6 - piece] * data[piece]
     f2s[...] = acc.reshape(32, DH).astype(BF16)
     f2r[z] = f2s[...]
     to_ring(send(1, lambda j: f2s, f2r.at[z]))
 
-    sub = iota((1, 8, DH), 1).astype(F32)
-    wide = jnp.concatenate(
-        [jnp.broadcast_to(idr[:, 2 + r : 3 + r, :], (PLANE, 8, DH)) + sub for r in range(NR)], axis=1
-    ).reshape(PLANE * 32, DH)
-    lanes = iota((1, DH), 1).astype(F32)
-    oh[:, 0:DH] = jnp.where(wide == lanes, 1.0, 0.0).astype(BF16)
-    oh[:, DH : 2 * DH] = jnp.where(wide == lanes + float(DH), 1.0, 0.0).astype(BF16)
+    inner(2)
 
     wait_all(g1r.at[pl.ds(0, PLANE - 1)], recv_sems, 3)
-    added = mm(oh[...], g1r[...].reshape(PLANE * 32, DH), 0, 0)
+    added = mm(oht[...], g1r[...].reshape(PLANE * 32, DH), 1, 0)
     g2s[...] = added.astype(BF16).reshape(RING, 32, DH)
     g2r[z] = g2s[z]
     to_ring(send(4, lambda j: g2s.at[j], g2r.at[z]))
@@ -242,21 +257,20 @@
     f3r[me] = f3s[me]
     to_plane(send(2, lambda j: f3s.at[j], f3r.at[me]))
 
-    after = jnp.zeros((8, DH), F32)
+    after = jnp.zeros((1, DH), F32)
     for piece in range(8):
         after = after + jnp.where(piece > a, idr[piece * 4 + quad], 0.0)
-    lane8 = iota((PIECE, 8), 1)
-    pfac[:, 0:8] = jnp.exp(suf + jnp.where(lane8 == 0, after[0:1, 0:1], after[1:2, 0:1]))
+    pfac[...] = jnp.exp(after)
 
     wait_all(g2r.at[pl.ds(0, RING - 1)], recv_sems, 4)
-    g3s[...] = jnp.sum(g2r[...].astype(F32), axis=0).reshape(4, 8, DH)
+    g3s[...] = jnp.sum(g2r[...].astype(F32), axis=0).reshape(4, 8, DH).astype(BF16)
     g3r[me] = g3s[quad]
     to_plane(send(5, lambda j: g3s.at[lax.rem(j, 4)], g3r.at[me]))
 
     inner(3)
 
     wait_all(g3r.at[pl.ds(0, PLANE - 1)], recv_sems, 5)
-    gfin[...] = g3r[...].reshape(H * DH, DH)
+    gfin[...] = g3r[...].astype(F32).reshape(H * DH, DH).astype(BF16)
 
     wait_all(f3r.at[pl.ds(0, PLANE - 1)], recv_sems, 2)
     got = f3r[...].astype(F32)
@@ -285,9 +299,9 @@
         ((NR, RMAX, H * DH), BF16),
         ((NR, RMAX, H * DH), BF16),
         ((NR, H * DH, DH), BF16),
-        ((H * DH, DH), F32),
+        ((H * DH, DH), BF16),
         ((CH, DH), F32),
-        ((PIECE, DH), F32),
+        ((1, DH), F32),
     )
     return pl.pallas_call(
         exchange_kernel,
@@ -304,12 +318,11 @@
             pltpu.VMEM((NR, H, RMAX), F32),
             pltpu.VMEM((NR, RMAX), jnp.int32),
             pltpu.VMEM((NR * 4, CH), F32),
-            pltpu.VMEM((8, DH), F32),
             pltpu.VMEM((NR, H, DH, DH), BF16),
-            pltpu.VMEM((PLANE, 8, DH), F32),
-            pltpu.VMEM((PLANE, 8, DH), F32),
-            pltpu.VMEM((8, DH), F32),
-            pltpu.VMEM((PLANE, 8, DH), F32),
+            pltpu.VMEM((PLANE, 8, DH), BF16),
+            pltpu.VMEM((PLANE, 8, DH), BF16),
+            pltpu.VMEM((1, DH), F32),
+            pltpu.VMEM((PLANE, 1, DH), F32),
             pltpu.VMEM((32, DH), BF16),
             pltpu.VMEM((RING, 32, DH), BF16),
             pltpu.VMEM((PLANE, 32, DH), BF16),
@@ -318,9 +331,10 @@
             pltpu.VMEM((PLANE, 32, DH), BF16),
             pltpu.VMEM((RING, 32, DH), BF16),
             pltpu.VMEM((RING, 32, DH), BF16),
-            pltpu.VMEM((4, 8, DH), F32),
-            pltpu.VMEM((PLANE, 8, DH), F32),
+            pltpu.VMEM((4, 8, DH), BF16),
+            pltpu.VMEM((PLANE, 8, DH), BF16),
             pltpu.VMEM((PLANE * 32, 2 * DH), BF16),
+            pltpu.VMEM((2 * DH, PLANE * 32), BF16),
             pltpu.SemaphoreType.DMA((12,)),
             pltpu.SemaphoreType.DMA((7,)),
             pltpu.SemaphoreType.DMA((7,)),
@@ -362,11 +376,10 @@
             early.append(c)
     for h in range(H):
         hs = HEADS[h]
-        factor = pfac[:, h : h + 1]
-        hi, lo = split(gfin[hs, :])
-        vh, kh = pv[0, :, hs], pk[0, :, hs]
-        pdk[0, :, hs] = (factor * (mm(vh, hi, 1, 1) + mm(vh, lo, 1, 1))).astype(BF16)
-        pdv[0, :, hs] = (factor * (mm(kh, hi, 1, 0) + mm(kh, lo, 1, 0))).astype(BF16)
+        factor = cols[:, 64 + h : 65 + h] * pfac[:, h : h + 1]
+        g = gfin[hs, :]
+        pdk[0, :, hs] = (factor * mm(pv[0, :, hs], g, 1, 1)).astype(BF16)
+        pdv[0, :, hs] = (factor * mm(pk[0, :, hs], g, 1, 0)).astype(BF16)
     for i, (s, d) in enumerate(((pdk, pdk_hbm), (pdv, pdv_hbm))):
         c = pltpu.make_async_copy(s, d, sems.at[10 + i])
         c.start()

time: 33.8 us -> 31 us (0.917)
  Pallas kernels: 33.1 us -> 30.2 us
    pallas_call x1, Pallas kernels: 30.9 us -> 28 us  [exchange(): pl.pallas_call(exchange_kernel, out_shape=tuple((pltpu.VMEM(s, t) for s,...]
where the time goes in v3:
time: 31 us; the launch traced here: 30.9 us
  Pallas kernels  30.2 us (97%)
  between operations  0.64 us (2%)
    pallas_call x1, Pallas kernels, exchange(): pl.pallas_call(exchange_kernel, out_shape=tuple((pltpu.VMEM(s, t) for s,...  28 us
    pallas_call x1, Pallas kernels, finish(): pl.pallas_call(finish_kernel, out_shape=(big,) * 4 + (small,) * 2, in_spe...  2.26 us

profile of v3, /device:TPU:1, one launch (start us, length us, event | category | flops | bytes accessed | tf_op | source)
XLA Modules:
  0.0 30.9 jit_solution(18100244174563627188)
XLA Ops:
  0.6 28.0 %exchange.1 = (bf16[1,256,256]{2,1,0:T(8,128)(2,1)S(1)}, bf16[1,256,256]{2,1,0:T(8,128)(2,1)S(1)}, bf16[4,512,256]{2,1,0:T(8,128)(2,1)S(1)}, bf16[4,512,256]{2,1...) custom-call(s32[4]{0:T(128)} %gid_hbm.1, ...), custom_call_target="tpu_custom_call" | custom-call | tf_op jit(solution)/shard_map/exchange/pallas_call | solution.py:306
  28.6 2.3 %finish.1 = (bf16[4,512,256]{2,1,0:T(8,128)(2,1)}, bf16[4,512,256]{2,1,0:T(8,128)(2,1)}, bf16[4,512,256]{2,1,0:T(8,128)(2,1)}, bf16[4,512,256]{2,1,0:T(8,128)(2,...) custom-call(bf16[1,256,256]{2,1,0:T(8,128)(2,1)S(1)} %get-tuple-element.18.pk, ...), custom_call_target="tpu_custom_call" | custom-call | tf_op jit(solution)/shard_map/finish/pallas_call | solution.py:396

commit v4 on v3

--- a/solution.py
+++ b/solution.py
@@ -79,7 +79,7 @@
             )
         )
     ]
-    for c in loads:
+    for c in loads[:8]:
         c.start()
 
     def to_plane(fn):
@@ -98,6 +98,8 @@
 
     to_plane(greet)
     to_ring(greet)
+    for c in loads[8:]:
+        c.start()
 
     def send(stage, src_of, dst):
         def one(j, dev):
@@ -117,10 +119,13 @@
 
     for c in loads[:5]:
         c.wait()
-    upper = (iota((CH, CH), 0) <= iota((CH, CH), 1)).astype(F32)
+    upper = jnp.where(iota((CH, CH), 0) <= iota((CH, CH), 1), 1.0, 0.0).astype(BF16)
     lane = iota((1, CH), 1)
     grows = jnp.concatenate([rg[r, :, t] for r in range(NR) for t in TOKENS] + [pg[0]], axis=0)
-    cums = mm(grows, upper, 1, 0, precision=HI)
+    high, rest = grows.astype(BF16), grows
+    rest = rest - high.astype(F32)
+    middle, low = split(rest)
+    cums = mm(high, upper, 1, 0) + (mm(middle, upper, 1, 0) + mm(low, upper, 1, 0))
     crows[...] = cums[: NR * 4]
     exps = jnp.exp(cums)
     tots = cums[:, CH - 1 : CH]
@@ -131,7 +136,12 @@
         opens = [jnp.where(lane + c * CH < lens[0, r], 1.0, 0.0) for c in range(len(TOKENS))]
         for on, t in zip(opens, TOKENS):
             rows.append(on * mask[r : r + 1, t].astype(F32) * (adv[r].astype(F32) * (1.0 / 1024.0)))
-        rows += [falls[4 * r : 4 * r + 2]] + opens + [jnp.zeros((2, CH), F32)]
+        fall = jnp.exp(tots[4 * r : 4 * r + 2])
+        rows += [
+            falls[4 * r : 4 * r + 2],
+            exps[4 * r : 4 * r + 2] * opens[0],
+            exps[4 * r + 2 : 4 * r + 4] * fall * opens[1],
+        ]
     rows += [falls[NR * 4 : NR * 4 + 2], jnp.zeros((62, CH), F32)]
     cols = jnp.concatenate(rows, axis=0).T
     cols_out[...] = cols
@@ -183,6 +193,7 @@
     loads[10].wait()
     loads[11].wait()
     causal = iota((CH, CH), 0) >= iota((CH, CH), 1)
+    place = iota((CH, DH), 0)
 
     def inner(r):
         for h in range(H):
@@ -208,7 +219,7 @@
                     e = col(cols, r, 4 + 2 * c + h)
                     out = out + e * mm(qc, step, 1, 0)
                     dq = dq + e * mm(gc, step, 1, 1)
-                pout[r, t, hs] = out
+                pout[r, t, hs] = jnp.where(place + c * CH < lens[0, r], out, 0.0)
                 pdq[r, t, hs] = dq
                 dk[r, t, hs] = dkc.astype(BF16)
                 dv[r, t, hs] = dvc.astype(BF16)
@@ -361,14 +372,9 @@
         for h in range(H):
             hs = HEADS[h]
             state = starts[r, hs, :]
-            span = None
             for c, t in enumerate(TOKENS):
-                e = col(cols, r, 4 + 2 * c + h)
-                if c == 1:
-                    e = e * span
-                span = e[CH - 1 : CH]
-                o = pout[r, t, hs] + e * mm(q[r, t, hs], state, 1, 0)
-                out[r, t, hs] = (o * col(cols, r, 12 + c)).astype(BF16)
+                e = col(cols, r, 12 + 2 * c + h)
+                out[r, t, hs] = (pout[r, t, hs] + e * mm(q[r, t, hs], state, 1, 0)).astype(BF16)
                 dq[r, t, hs] = (pdq[r, t, hs] + e * mm(go[r, t, hs], state, 1, 1)).astype(BF16)
         for i, (s, d) in enumerate(((out, out_hbm), (dq, dq_hbm))):
             c = pltpu.make_async_copy(s.at[r], d.at[r], sems.at[2 + 2 * r + i])

time: 31 us -> 30.9 us (level)
  no operation moved by 1% of the time
where the time goes in v4:
time: 30.9 us; the launch traced here: 30.8 us
  Pallas kernels  30.2 us (98%)
  between operations  0.64 us (2%)
    pallas_call x1, Pallas kernels, exchange(): pl.pallas_call(exchange_kernel, out_shape=tuple((pltpu.VMEM(s, t) for s,...  28 us
    pallas_call x1, Pallas kernels, finish(): pl.pallas_call(finish_kernel, out_shape=(big,) * 4 + (small,) * 2, in_spe...  2.18 us

profile of v4, /device:TPU:1, one launch (start us, length us, event | category | flops | bytes accessed | tf_op | source)
XLA Modules:
  0.0 30.8 jit_solution(7416507292198082621)
XLA Ops:
  0.6 28.0 %exchange.1 = (bf16[1,256,256]{2,1,0:T(8,128)(2,1)S(1)}, bf16[1,256,256]{2,1,0:T(8,128)(2,1)S(1)}, bf16[4,512,256]{2,1,0:T(8,128)(2,1)S(1)}, bf16[4,512,256]{2,1...) custom-call(s32[4]{0:T(128)} %gid_hbm.1, ...), custom_call_target="tpu_custom_call" | custom-call | tf_op jit(solution)/shard_map/exchange/pallas_call | solution.py:317
  28.6 2.2 %finish.1 = (bf16[4,512,256]{2,1,0:T(8,128)(2,1)}, bf16[4,512,256]{2,1,0:T(8,128)(2,1)}, bf16[4,512,256]{2,1,0:T(8,128)(2,1)}, bf16[4,512,256]{2,1,0:T(8,128)(2,...) custom-call(bf16[1,256,256]{2,1,0:T(8,128)(2,1)S(1)} %get-tuple-element.18.pk, ...), custom_call_target="tpu_custom_call" | custom-call | tf_op jit(solution)/shard_map/finish/pallas_call | solution.py:402
